TPU v7x, 32 devices: a whole 2x2x4 slice. The times are simulated.
32 devices in a mesh: head: 4 (over y, core), shard: 8 (over z, x).
Axes of the slice: x: 2, y: 2, z: 4, core: 2. Of those that a mesh axis runs over, the one named last changes fastest.
Arguments:
- inputs: bfloat16 [4, 8, 4, 64, 2048], P(None, 'shard', 'head'), may hold values from -6 to 6
- segments: int32 [4, 8, 4, 64], P(None, 'shard'), may hold values from 0 to 2047, as said below
- query_weight: bfloat16 [2048, 256], P(('head', 'shard')), may hold values from -0.125 to 0.125
- key_weight: bfloat16 [2048, 256], P(('head', 'shard')), may hold values from -0.125 to 0.125
- value_weight: bfloat16 [2048, 2048], P(('head', 'shard')), may hold values from -0.125 to 0.125
- project_weight: bfloat16 [2048, 2048], P(('head', 'shard')), may hold values from -1.5 to 1.5
- attend_gain: bfloat16 [2048], P(('head', 'shard')), may hold values from 0.5 to 1.5
- gate_weight: bfloat16 [2048, 5632], P('shard', 'head'), may hold values from -0.125 to 0.125
- up_weight: bfloat16 [2048, 5632], P('shard', 'head'), may hold values from -0.125 to 0.125
- down_weight: bfloat16 [5632, 2048], P('head', 'shard'), may hold values from -0.078125 to 0.078125
- forward_gain: bfloat16 [2048], P(('head', 'shard')), may hold values from 0.5 to 1.5
- upstream: bfloat16 [4, 8, 4, 64, 2048], P(None, 'shard', 'head'), may hold values from -6 to 6
Outputs:
- outputs: bfloat16 [4, 8, 4, 64, 2048], P(None, 'shard', 'head')
- inputs_grad: float32 [4, 8, 4, 64, 2048], P(None, 'shard', 'head')
- query_grad: float32 [2048, 256], P(('head', 'shard'))
- key_grad: float32 [2048, 256], P(('head', 'shard'))
- value_grad: float32 [2048, 2048], P(('head', 'shard'))
- project_grad: float32 [2048, 2048], P(('head', 'shard'))
- attend_grad: float32 [2048], P(('head', 'shard'))
- gate_grad: float32 [2048, 5632], P('shard', 'head')
- up_grad: float32 [2048, 5632], P('shard', 'head')
- down_grad: float32 [5632, 2048], P('head', 'shard')
- forward_grad: float32 [2048], P(('head', 'shard'))
Inputs may be any that keep to these rules, and one draw needn't show every extreme that they name: `segments`: A token's segment number is the position within its sequence of the first token of its document, so the numbers start at 0 and never fall from one token to the next; one of the 4 sequences is a single document, and another ends with a document of one token.
All inputs are finite; a program needn't handle non-finite values.
Results may differ from a plain program's by a relative error of at most 0.017.
Values may be sent and summed in bfloat16 or wider, within the bound.
No kernel may reach another device: no remote copies, remote signals or barrier semaphores. Data moves between devices by JAX's collectives and lax.ppermute only.
A program may use at most 576 MiB of HBM per device.

v0:
```python
import math
import jax
import jax.numpy as jnp
from jax import lax
from jax.sharding import PartitionSpec as P

D = 2048
HEADS = 16
QK = 16
VD = 128
EPS_NORM = 1e-05
HIGH = lax.Precision.HIGHEST


def carried_in(value, axis, combine, identity):
    size, here = (lax.axis_size(axis), lax.axis_index(axis))
    everything = jax.tree.map(lambda part: lax.all_gather(part, axis), value)
    start = jax.tree.map(
        lambda part, zero: jnp.broadcast_to(jnp.asarray(zero, part.dtype), part.shape),
        value,
        identity,
    )

    def carried_turn(k, before):
        reached = k < here
        new = combine(before, jax.tree.map(lambda part: part[k], everything))
        return jax.tree.map(lambda a, b: jnp.where(reached, a, b), new, before)

    return lax.fori_loop(0, size, carried_turn, start)


def prefix(value, axis, combine, identity):
    size, here = (lax.axis_size(axis), lax.axis_index(axis))
    everything = jax.tree.map(
        lambda part, kind: lax.all_gather(part.astype(kind), axis),
        value,
        jax.tree.map(lambda a: jnp.bfloat16 if a.dtype == jnp.float32 else a.dtype, value),
    )
    start = jax.tree.map(
        lambda part, zero: jnp.broadcast_to(jnp.asarray(zero, part.dtype), part.shape),
        value,
        identity,
    )

    def prefix_turn(k, before):
        at = size - 1 - k
        reached = at > here
        new = combine(
            before, jax.tree.map(lambda part, own: part[at].astype(own.dtype), everything, value)
        )
        return jax.tree.map(lambda a, b: jnp.where(reached, a, b), new, before)

    return lax.fori_loop(0, size, prefix_turn, start)


def features(values):
    qk_size = values.shape[-1]
    square = (values[..., :, None] * values[..., None, :]).reshape(
        values.shape[:-1] + (qk_size * qk_size,)
    )
    ones_col = jnp.ones(values.shape[:-1] + (1,), jnp.float32)
    return jnp.concatenate(
        [ones_col, values * qk_size ** (-0.25), square / math.sqrt(2.0 * qk_size)], axis=-1
    )


def features_back(values, grad_feats):
    qk_size = values.shape[-1]
    linear = grad_feats[..., 1 : 1 + qk_size]
    square = grad_feats[..., 1 + qk_size :].reshape(grad_feats.shape[:-1] + (qk_size, qk_size))
    paired = jnp.einsum("...ij,...j->...i", square, values, precision=HIGH) + jnp.einsum(
        "...ji,...j->...i", square, values, precision=HIGH
    )
    return linear * qk_size ** (-0.25) + paired / math.sqrt(2.0 * qk_size)


def normalize(rows_in):
    inverse = lax.rsqrt(jnp.mean(rows_in * rows_in, axis=-1, keepdims=True) + EPS_NORM)
    return (rows_in * inverse, inverse)


def normalize_back(normed, inverse, grad_normed):
    return inverse * (grad_normed - normed * jnp.mean(grad_normed * normed, axis=-1, keepdims=True))


def forward_combine(earlier, latter):
    keep_old = (latter[2] <= earlier[2]).astype(jnp.float32)
    return (
        latter[0] + keep_old[..., None, None, None] * earlier[0],
        latter[1] + keep_old[..., None, None] * earlier[1],
        jnp.maximum(earlier[2], latter[2]),
    )


def backward_combine(earlier, latter):
    keep_old = (earlier[2] <= latter[2]).astype(jnp.float32)
    return (
        latter[0] + keep_old[..., None, None, None] * earlier[0],
        latter[1] + keep_old[..., None, None] * earlier[1],
        jnp.minimum(earlier[2], latter[2]),
    )


def product(left, right):
    return jnp.dot(left, right, preferred_element_type=jnp.float32)


def contract(pattern, left, right):
    return jnp.einsum(pattern, left, right, precision=HIGH)


def swiglu_pass(active_rows, grad_rows, gate_mat, up_mat, down_mat):
    gate_pre = product(active_rows, gate_mat)
    up_pre = product(active_rows, up_mat)
    sigmoid_gate = jax.nn.sigmoid(gate_pre)
    silu_gate = gate_pre * sigmoid_gate
    hidden_act = (silu_gate * up_pre).astype(jnp.bfloat16)
    down_out = product(hidden_act, down_mat)
    grad_hidden = product(grad_rows, down_mat.T)
    grad_gate = (
        grad_hidden * up_pre * (sigmoid_gate * (1.0 + gate_pre * (1.0 - sigmoid_gate)))
    ).astype(jnp.bfloat16)
    grad_up = (grad_hidden * silu_gate).astype(jnp.bfloat16)
    down_sum = product(hidden_act.T, grad_rows)
    gate_sum = product(active_rows.T, grad_gate)
    up_sum = product(active_rows.T, grad_up)
    grad_active = product(grad_gate, gate_mat.T) + product(grad_up, up_mat.T)
    return (down_out, grad_active, gate_sum, up_sum, down_sum)


def body(
    inputs,
    segments,
    query_weight,
    key_weight,
    value_weight,
    project_weight,
    attend_gain,
    gate_weight,
    up_weight,
    down_weight,
    forward_gain,
    upstream,
):
    groups = lax.axis_size("head")
    per_group = HEADS // groups
    seq_count = inputs.shape[0]
    sub_rows = inputs.shape[3]
    block_len = groups * sub_rows
    token_rows = seq_count * sub_rows
    root_qk = math.sqrt(QK)
    attend_set = (
        lax.all_gather(query_weight, ("head", "shard"), axis=0, tiled=True),
        lax.all_gather(key_weight, ("head", "shard"), axis=0, tiled=True),
        lax.all_gather(value_weight, ("head", "shard"), axis=0, tiled=True),
        lax.all_gather(project_weight, ("head", "shard"), axis=0, tiled=True),
        lax.all_gather(attend_gain, ("head", "shard"), axis=0, tiled=True),
        lax.all_gather(forward_gain, ("head", "shard"), axis=0, tiled=True),
    )
    full_query, full_key, full_value, full_project, full_gain_one, full_gain_two = attend_set
    hidden_in = inputs.reshape(token_rows, D).astype(jnp.float32)
    normed_one, inverse_one = normalize(hidden_in)
    gain_one = full_gain_one.astype(jnp.float32)
    active_one = (normed_one * gain_one).astype(jnp.bfloat16)
    query_rows = product(active_one, full_query).astype(jnp.bfloat16)
    key_rows = product(active_one, full_key).astype(jnp.bfloat16)
    value_rows = product(active_one, full_value).astype(jnp.bfloat16)

    def to_groups(rows_in):
        return rows_in.reshape(seq_count, 1, 1, sub_rows, rows_in.shape[-1])

    def to_heads(shards, head_size):
        return (
            shards.reshape(seq_count, block_len, per_group, head_size)
            .transpose(0, 2, 1, 3)
            .astype(jnp.float32)
        )

    def from_heads(head_arr):
        return (
            head_arr.astype(jnp.bfloat16)
            .transpose(0, 2, 1, 3)
            .reshape(seq_count, 1, groups, sub_rows, per_group * head_arr.shape[-1])
        )

    query_parts, key_parts, value_parts = (
        lax.all_to_all(to_groups(query_rows), "head", split_axis=4, concat_axis=2, tiled=True),
        lax.all_to_all(to_groups(key_rows), "head", split_axis=4, concat_axis=2, tiled=True),
        lax.all_to_all(to_groups(value_rows), "head", split_axis=4, concat_axis=2, tiled=True),
    )
    query_head = to_heads(query_parts, QK)
    key_head = to_heads(key_parts, QK)
    value_head = to_heads(value_parts, VD)
    seg_float = segments.reshape(seq_count, block_len).astype(jnp.float32)
    causal = lax.broadcasted_iota(jnp.int32, (block_len, block_len), 0) >= lax.broadcasted_iota(
        jnp.int32, (block_len, block_len), 1
    )
    visible = (causal[None] & (seg_float[:, :, None] == seg_float[:, None, :])).astype(jnp.float32)[
        :, None
    ]
    scores = contract("bhtd,bhsd->bhts", query_head, key_head) / root_qk
    weights = (1.0 + scores + 0.5 * scores * scores) * visible
    feat_query = features(query_head)
    feat_key = features(key_head)
    last_seg = seg_float[:, -1]
    last_mask = (seg_float == last_seg[:, None]).astype(jnp.float32)[:, None, :, None]
    masked_key = feat_key * last_mask
    state_local = contract("bhtf,bhtc->bhfc", masked_key, value_head)
    norm_local = jnp.sum(masked_key, axis=2)
    start_state = (
        jnp.zeros_like(state_local),
        jnp.zeros_like(norm_local),
        jnp.full_like(last_seg, -1.0),
    )
    state_in, norm_in, last_in = carried_in(
        (state_local, norm_local, last_seg), "shard", forward_combine, start_state
    )
    use_in = (seg_float == last_in[:, None]).astype(jnp.float32)[:, None, :, None]
    numerator = contract("bhts,bhsc->bhtc", weights, value_head) + use_in * contract(
        "bhtf,bhfc->bhtc", feat_query, state_in
    )
    denominator = jnp.sum(weights, axis=-1) + use_in[..., 0] * contract(
        "bhtf,bhf->bht", feat_query, norm_in
    )
    attended = numerator / denominator[..., None]
    mixed_rows = lax.all_to_all(
        from_heads(attended), "head", split_axis=2, concat_axis=4, tiled=True
    ).reshape(token_rows, HEADS * VD)
    attend_out = product(mixed_rows, full_project)
    residual = hidden_in + attend_out
    rows_gate, rows_up, rows_down = (
        lax.all_gather(gate_weight, "shard", axis=0, tiled=True),
        lax.all_gather(up_weight, "shard", axis=0, tiled=True),
        lax.all_gather(down_weight, "shard", axis=1, tiled=True),
    )
    normed_two, inverse_two = normalize(residual)
    gain_two = full_gain_two.astype(jnp.float32)
    active_two = (normed_two * gain_two).astype(jnp.bfloat16)
    grad_out = upstream.reshape(token_rows, D)
    full_gate, full_up, full_down = (
        lax.all_gather(rows_gate, "head", axis=1, tiled=True),
        lax.all_gather(rows_up, "head", axis=1, tiled=True),
        lax.all_gather(rows_down, "head", axis=0, tiled=True),
    )
    down_out, grad_active_two, gate_whole, up_whole, down_whole = swiglu_pass(
        active_two, grad_out, full_gate, full_up, full_down
    )
    gate_part, up_part, down_part = (
        lax.psum_scatter(
            gate_whole.astype(jnp.bfloat16), "head", scatter_dimension=1, tiled=True
        ).astype(jnp.float32),
        lax.psum_scatter(
            up_whole.astype(jnp.bfloat16), "head", scatter_dimension=1, tiled=True
        ).astype(jnp.float32),
        lax.psum_scatter(
            down_whole.astype(jnp.bfloat16), "head", scatter_dimension=0, tiled=True
        ).astype(jnp.float32),
    )
    result = residual + down_out
    outputs = result.astype(jnp.bfloat16).reshape(inputs.shape)
    gate_grad, up_grad, down_grad = (
        lax.psum_scatter(
            gate_part.astype(jnp.bfloat16), "shard", scatter_dimension=0, tiled=True
        ).astype(jnp.float32),
        lax.psum_scatter(
            up_part.astype(jnp.bfloat16), "shard", scatter_dimension=0, tiled=True
        ).astype(jnp.float32),
        lax.psum_scatter(
            down_part.astype(jnp.bfloat16), "shard", scatter_dimension=1, tiled=True
        ).astype(jnp.float32),
    )
    gain_two_sum = jnp.sum(grad_active_two * normed_two, axis=0)
    grad_resid = grad_out.astype(jnp.float32) + normalize_back(
        normed_two, inverse_two, grad_active_two * gain_two
    )
    grad_attend = grad_resid.astype(jnp.bfloat16)
    project_sum = product(mixed_rows.T, grad_attend)
    grad_mixed = product(grad_attend, full_project.T).astype(jnp.bfloat16)
    grad_parts = lax.all_to_all(
        to_groups(grad_mixed), "head", split_axis=4, concat_axis=2, tiled=True
    )
    grad_head = to_heads(grad_parts, VD)
    grad_numer = grad_head / denominator[..., None]
    grad_denom = -jnp.sum(grad_head * attended, axis=-1) / denominator
    grad_value = contract("bhts,bhtc->bhsc", weights, grad_numer)
    grad_weights = contract("bhtc,bhsc->bhts", grad_numer, value_head) + grad_denom[..., None]
    grad_scores = grad_weights * (1.0 + scores) * visible
    grad_query = contract("bhts,bhsd->bhtd", grad_scores, key_head) / root_qk
    grad_key = contract("bhts,bhtd->bhsd", grad_scores, query_head) / root_qk
    grad_feat_query = use_in * (
        contract("bhtc,bhfc->bhtf", grad_numer, state_in)
        + grad_denom[..., None] * norm_in[:, :, None, :]
    )
    grad_state_in = contract("bhtf,bhtc->bhfc", feat_query, use_in * grad_numer)
    grad_norm_in = contract("bhtf,bht->bhf", feat_query, use_in[..., 0] * grad_denom)
    end_state = (
        jnp.zeros_like(grad_state_in),
        jnp.zeros_like(grad_norm_in),
        jnp.full_like(last_in, 1000000000.0),
    )
    grad_state_out, grad_norm_out, unused_keys = prefix(
        (grad_state_in, grad_norm_in, last_in), "shard", backward_combine, end_state
    )
    grad_feat_key = last_mask * (
        contract("bhfc,bhtc->bhtf", grad_state_out, value_head) + grad_norm_out[:, :, None, :]
    )
    grad_value = grad_value + last_mask * contract("bhtf,bhfc->bhtc", feat_key, grad_state_out)
    grad_query = grad_query + features_back(query_head, grad_feat_query)
    grad_key = grad_key + features_back(key_head, grad_feat_key)
    query_back, key_back, value_back = (
        lax.all_to_all(from_heads(grad_query), "head", split_axis=2, concat_axis=4, tiled=True),
        lax.all_to_all(from_heads(grad_key), "head", split_axis=2, concat_axis=4, tiled=True),
        lax.all_to_all(from_heads(grad_value), "head", split_axis=2, concat_axis=4, tiled=True),
    )
    query_back = query_back.reshape(token_rows, HEADS * QK)
    key_back = key_back.reshape(token_rows, HEADS * QK)
    value_back = value_back.reshape(token_rows, HEADS * VD)
    query_sum = product(active_one.T, query_back)
    key_sum = product(active_one.T, key_back)
    value_sum = product(active_one.T, value_back)
    grad_active_one = (
        product(query_back, full_query.T)
        + product(key_back, full_key.T)
        + product(value_back, full_value.T)
    )
    gain_one_sum = jnp.sum(grad_active_one * normed_one, axis=0)
    query_grad, key_grad, value_grad, project_grad, attend_grad, forward_grad = (
        lax.psum_scatter(query_sum, ("head", "shard"), scatter_dimension=0, tiled=True),
        lax.psum_scatter(key_sum, ("head", "shard"), scatter_dimension=0, tiled=True),
        lax.psum_scatter(value_sum, ("head", "shard"), scatter_dimension=0, tiled=True),
        lax.psum_scatter(project_sum, ("head", "shard"), scatter_dimension=0, tiled=True),
        lax.psum_scatter(gain_one_sum, ("head", "shard"), scatter_dimension=0, tiled=True),
        lax.psum_scatter(gain_two_sum, ("head", "shard"), scatter_dimension=0, tiled=True),
    )
    inputs_grad = (
        grad_resid + normalize_back(normed_one, inverse_one, grad_active_one * gain_one)
    ).reshape(inputs.shape)
    return (
        outputs,
        inputs_grad,
        query_grad,
        key_grad,
        value_grad,
        project_grad,
        attend_grad,
        gate_grad,
        up_grad,
        down_grad,
        forward_grad,
    )


def solution(mesh):
    in_specs = (
        P(None, "shard", "head", None, None),
        P(None, "shard", None, None),
        P(("head", "shard"), None),
        P(("head", "shard"), None),
        P(("head", "shard"), None),
        P(("head", "shard"), None),
        P(("head", "shard")),
        P("shard", "head"),
        P("shard", "head"),
        P("head", "shard"),
        P(("head", "shard")),
        P(None, "shard", "head", None, None),
    )
    out_specs = (
        P(None, "shard", "head", None, None),
        P(None, "shard", "head", None, None),
        P(("head", "shard"), None),
        P(("head", "shard"), None),
        P(("head", "shard"), None),
        P(("head", "shard"), None),
        P(("head", "shard")),
        P("shard", "head"),
        P("shard", "head"),
        P("head", "shard"),
        P(("head", "shard")),
    )
    return jax.shard_map(body, mesh=mesh, in_specs=in_specs, out_specs=out_specs, check_vma=False)
```

profile of v0, /device:TPU:0, one launch (start us, length us, event | category | flops | bytes accessed | tf_op | source)
XLA Modules:
  0.0 3412.9 jit_solution(4737021666080043786)
XLA Ops:
  12.9 42.1 %all-reduce.7 = (bf16[2048]{0:T(1024)(128)(2,1)S(1)}, bf16[2048]{0:T(1024)(128)(2,1)S(1)}) all-reduce(bf16[2048]{0:T(1024)(128)(2,1)S(1)} %dynamic-update-slice, bf16[2048]{0:T(1024)(128)(2,1)S(1)} %dynamic-update-slice.2), channel_id=1, replica_groups=mesh['head'=4,'shard'=8] {'head','shard'}, use_global_device_ids=true, to_apply=%add | all-reduce | flops 4096 | bytes 16384
  58.4 9.2 all-gather.21.cloned.1.call-done
  78.9 68.0 %all-gather.23.cloned.1.call-done = bf16[2048,2048]{1,0:T(8,128)(2,1)} async-done(((bf16[64,2048]{1,0:T(8,128)(2,1)}), bf16[2048,2048]{1,0:T(8,128)(2,1)}) %all-gather.23.cloned.1.call-update) | async-done | bytes 8388624 | tf_op jit(solution)/shard_map/all_gather | solution.py:155
  169.3 11.6 all-to-all-done.2
  205.7 34.7 %all-gather.27.cloned.1.call-done = bf16[2048,1408]{1,0:T(8,128)(2,1)} async-done(((bf16[256,1408]{1,0:T(8,128)(2,1)}), bf16[2048,1408]{1,0:T(8,128)(2,1)}) %all-gather.27.cloned.1.call-update) | async-done | bytes 5767184 | tf_op jit(solution)/shard_map/all_gather | solution.py:232
  240.5 92.8 %all-gather.31.cloned.1.call-done = bf16[2048,1408]{1,0:T(8,128)(2,1)} async-done(((bf16[256,1408]{1,0:T(8,128)(2,1)}), bf16[2048,1408]{1,0:T(8,128)(2,1)}) %all-gather.31.cloned.1.call-update) | async-done | bytes 5767184 | tf_op jit(solution)/shard_map/all_gather | solution.py:233
  333.4 93.6 %all-gather.35.cloned.1.call-done = bf16[1408,2048]{1,0:T(8,128)(2,1)} async-done(((bf16[1408,256]{1,0:T(8,128)(2,1)}), bf16[1408,2048]{1,0:T(8,128)(2,1)}) %all-gather.35.cloned.1.call-update) | async-done | bytes 5767184 | tf_op jit(solution)/shard_map/all_gather | solution.py:234
  429.5 52.3 %all-gather.19.cloned.1.call-done = bf16[2048,256]{1,0:T(8,128)(2,1)} async-done(((bf16[64,256]{1,0:T(8,128)(2,1)}), bf16[2048,256]{1,0:T(8,128)(2,1)}) %all-gather.19.cloned.1.call-update) | async-done | bytes 1048592 | tf_op jit(solution)/shard_map/all_gather | solution.py:153
  488.1 39.4 %all-reduce.1 = f32[32]{0:T(128)S(1)} all-reduce(f32[32]{0:T(128)S(1)} %bitcast_dynamic-update-slice_fusion), channel_id=3, replica_groups=mesh['head'=4,'shard'=8] {'shard'}, use_global_device_ids=true, to_apply=%add.1 | all-reduce | flops 32 | bytes 256
  534.9 39.2 %all-gather.2 = f32[32,4,273]{2,1,0:T(4,128)} all-gather(f32[4,4,273]{2,1,0:T(4,128)S(1)} %multiply_reduce_fusion), channel_id=4, replica_groups=mesh['head'=4,'shard'=8] {'shard'}, dimensions={0}, use_global_device_ids=true | all-gather | bytes 157248 | tf_op jit(solution)/shard_map/all_gather | solution.py:17
  584.6 246.1 %all-gather.39.cloned.1.call-done = f32[32,4,273,128]{3,1,2,0:T(4,128)} async-done(((f32[4,4,273,128]{3,1,2,0:T(4,128)}), f32[32,4,273,128]{3,1,2,0:T(4,128)}) %all-gather.39.cloned.1.call-update) | async-done | bytes 17891344 | tf_op jit(solution)/shard_map/all_gather | solution.py:17
  830.7 29.9 while.38
  867.4 8.5 fusion.18
  885.2 24.2 all-to-all-done.3
  911.5 8.9 all-gather.25.cloned.1.call-done
  926.9 138.3 %all-gather.29.cloned.1.call-done = bf16[2048,5632]{1,0:T(8,128)(2,1)} async-done(((bf16[2048,1408]{1,0:T(8,128)(2,1)}), bf16[2048,5632]{1,0:T(8,128)(2,1)}) %all-gather.29.cloned.1.call-update) | async-done | bytes 23068688 | tf_op jit(solution)/shard_map/all_gather | solution.py:241
  1065.2 14.6 fusion.61
  1079.8 130.0 %all-gather.33.cloned.1.call-done = bf16[2048,5632]{1,0:T(8,128)(2,1)} async-done(((bf16[2048,1408]{1,0:T(8,128)(2,1)}), bf16[2048,5632]{1,0:T(8,128)(2,1)}) %all-gather.33.cloned.1.call-update) | async-done | bytes 23068688 | tf_op jit(solution)/shard_map/all_gather | solution.py:242
  1209.8 14.3 fusion.62
  1224.0 130.5 %all-gather.37.cloned.1.call-done = bf16[5632,2048]{1,0:T(8,128)(2,1)} async-done(((bf16[1408,2048]{1,0:T(8,128)(2,1)}), bf16[5632,2048]{1,0:T(8,128)(2,1)}) %all-gather.37.cloned.1.call-update) | async-done | bytes 23068688 | tf_op jit(solution)/shard_map/all_gather | solution.py:243
  1354.6 17.4 multiply_convert_fusion
  1373.5 11.0 convolution_convert_fusion.2
  1384.6 30.6 copy.215
  1415.3 17.6 convolution_convert_fusion.1
  1432.9 30.1 copy.217
  1464.2 13.1 convolution_convert_fusion
  1477.4 13.2 fusion.63
  1490.6 13.5 multiply_reduce_fusion.5
  1516.2 29.6 all_to_all.114
  1568.5 24.9 reduce-scatter.31.cloned.1.call-done
  1601.8 161.2 %reduce-scatter.33.cloned.1.call-done = bf16[1408,2048]{1,0:T(8,128)(2,1)} async-done(((bf16[5632,2048]{1,0:T(8,128)(2,1)}), bf16[1408,2048]{1,0:T(8,128)(2,1)}) %reduce-scatter.33.cloned.1.call-update) | async-done | bytes 5767184
  1763.0 8.3 copy.218
  1771.4 160.8 %reduce-scatter.27.cloned.1.call-done = bf16[1408,2048]{1,0:T(8,128)(2,1)} async-done(((bf16[5632,2048]{1,0:T(8,128)(2,1)}), bf16[1408,2048]{1,0:T(8,128)(2,1)}) %reduce-scatter.27.cloned.1.call-update) | async-done | bytes 5767184 | tf_op jit(solution)/shard_map/reduce_scatter | solution.py:255
  1933.9 21.9 all-reduce.3
  1991.1 33.3 all-gather.5
  2030.2 38.9 %all-gather.41.cloned.1.call-done = bf16[32,4,273,128]{3,1,2,0:T(4,128)(2,1)} async-done(((bf16[4,4,273,128]{3,1,2,0:T(4,128)(2,1)}), bf16[32,4,273,128]{3,1,2,0:T(4,128)(2,1)}) %all-gather.41.cloned.1.call-update) | async-done | bytes 8945680 | tf_op jit(solution)/shard_map/all_gather | solution.py:35
  2069.1 28.2 while.39
  2125.3 10.0 fusion.37
  2135.7 12.6 fusion.13
  2154.4 17.1 all_to_all.116
  2183.3 12.5 fusion.12
  2204.4 41.0 %all-reduce.6 = (f32[2048]{0:T(1024)S(1)}, f32[2048]{0:T(1024)S(1)}) all-reduce(f32[2048]{0:T(1024)S(1)} %get-tuple-element.499, f32[2048]{0:T(1024)S(1)} %get-tuple-element.497), channel_id=12, replica_groups=mesh['head'=4,'shard'=8] {'head','shard'}, use_global_device_ids=true, to_apply=%region_16.17.clone | all-reduce | flops 4096 | bytes 32768
  2252.4 44.2 %reduce-scatter.25.cloned.1.call-done = bf16[256,1408]{1,0:T(8,128)(2,1)} async-done(((bf16[2048,1408]{1,0:T(8,128)(2,1)}), bf16[256,1408]{1,0:T(8,128)(2,1)}) %reduce-scatter.25.cloned.1.call-update) | async-done | bytes 720912 | tf_op jit(solution)/shard_map/reduce_scatter | solution.py:265
  2298.8 111.9 %reduce-scatter.29.cloned.1.call-done = bf16[1408,256]{1,0:T(8,128)(2,1)} async-done(((bf16[1408,2048]{1,0:T(8,128)(2,1)}), bf16[1408,256]{1,0:T(8,128)(2,1)}) %reduce-scatter.29.cloned.1.call-update) | async-done | bytes 720912 | tf_op jit(solution)/shard_map/reduce_scatter | solution.py:268
  2413.0 138.0 %reduce-scatter.15.cloned.1.call-done = f32[64,256]{1,0:T(8,128)} async-done(((f32[2048,256]{1,0:T(8,128)}), f32[64,256]{1,0:T(8,128)}) %reduce-scatter.15.cloned.1.call-update) | async-done | bytes 65552 | tf_op jit(solution)/shard_map/reduce_scatter | solution.py:328
  2551.1 137.0 %reduce-scatter.17.cloned.1.call-done = f32[64,256]{1,0:T(8,128)} async-done(((f32[2048,256]{1,0:T(8,128)}), f32[64,256]{1,0:T(8,128)}) %reduce-scatter.17.cloned.1.call-update) | async-done | bytes 65552 | tf_op jit(solution)/shard_map/reduce_scatter | solution.py:329
  2688.1 357.4 %reduce-scatter.21.cloned.1.call-done = f32[64,2048]{1,0:T(8,128)} async-done(((f32[2048,2048]{1,0:T(8,128)}), f32[64,2048]{1,0:T(8,128)}) %reduce-scatter.21.cloned.1.call-update) | async-done | bytes 524304 | tf_op jit(solution)/shard_map/reduce_scatter | solution.py:331
  3045.5 360.4 %reduce-scatter.19.cloned.1.call-done = f32[64,2048]{1,0:T(8,128)} async-done(((f32[2048,2048]{1,0:T(8,128)}), f32[64,2048]{1,0:T(8,128)}) %reduce-scatter.19.cloned.1.call-update) | async-done | bytes 524304 | tf_op jit(solution)/shard_map/reduce_scatter | solution.py:330
  (396 shorter events, 329.7 us)
Async XLA Ops:
  7.2 50.9 %copy-start.2 = (bf16[4,1,1,64,2048]{4,3,2,1,0:T(8,128)(2,1)S(1)}, bf16[4,1,1,64,2048]{4,3,2,1,0:T(8,128)(2,1)}, u32[]{:S(2)}) copy-start(bf16[4,1,1,64,2048]{4,3,2,1,0:T(8,128)(2,1)} %param.16) | copy-start | bytes 3145732
  7.2 60.4 %all-gather.21.cloned.1.call-start = ((), (), s32[]{:S(2)}) async-start(), calls=%async_computation.19 | async-start | bytes 1081344 | tf_op jit(solution)/shard_map/all_gather | solution.py:154
  7.9 139.1 %all-gather.23.cloned.1.call-start = ((), (), s32[]{:S(2)}) async-start(), calls=%async_computation.20 | async-start | bytes 8650752 | tf_op jit(solution)/shard_map/all_gather | solution.py:155
  8.7 231.8 %all-gather.27.cloned.1.call-start = ((), (), s32[]{:S(2)}) async-start(), calls=%async_computation.22 | async-start | bytes 6488064 | tf_op jit(solution)/shard_map/all_gather | solution.py:232
  9.4 323.9 %all-gather.31.cloned.1.call-start = ((), (), s32[]{:S(2)}) async-start(), calls=%async_computation.24 | async-start | bytes 6488064 | tf_op jit(solution)/shard_map/all_gather | solution.py:233
  10.0 417.0 %all-gather.35.cloned.1.call-start = ((), (), s32[]{:S(2)}) async-start(), calls=%async_computation.26 | async-start | bytes 6488064 | tf_op jit(solution)/shard_map/all_gather | solution.py:234
  10.6 471.3 %all-gather.19.cloned.1.call-start = ((), (), s32[]{:S(2)}) async-start(), calls=%async_computation.18 | async-start | bytes 1081344 | tf_op jit(solution)/shard_map/all_gather | solution.py:153
  57.1 96.5 %copy-start.62 = (f32[256]{0:T(256)}, f32[256]{0:T(256)S(1)}, u32[]{:S(2)}) copy-start(f32[256]{0:T(256)S(1)} %rsqrt.21) | copy-start | bytes 3076
  70.3 7.9 all-to-all-start.1
  73.8 457.8 %copy-start.52 = (f32[4,256]{1,0:T(4,128)}, f32[4,256]{1,0:T(4,128)S(1)}, u32[]{:S(2)}) copy-start(f32[4,256]{1,0:T(4,128)S(1)} %compare_convert_fusion.3) | copy-start | bytes 12292
  73.8 793.6 %copy-start.58 = (f32[273]{0:T(512)}, f32[273]{0:T(512)S(1)}, u32[]{:S(2)}) copy-start(f32[273]{0:T(512)S(1)} %pad.3.clone) | copy-start | bytes 3280
  78.9 87.7 %copy-start.39 = (bf16[4,256,4,16]{1,3,2,0:T(8,128)(2,1)}, bf16[4,256,4,16]{1,3,2,0:T(8,128)(2,1)S(1)}, u32[]{:S(2)}) copy-start(bf16[4,256,4,16]{1,3,2,0:T(8,128)(2,1)S(1)} %reshape.281) | copy-start | bytes 393220
  162.1 18.8 all-to-all-start.2
  166.4 664.4 %all-gather.39.cloned.1.call-start = ((), (), s32[]{:S(2)}) async-start(), calls=%async_computation.36 | async-start | bytes 20127744 | tf_op jit(solution)/shard_map/all_gather | solution.py:17
  166.6 23.0 copy-start.19
  166.7 30.8 copy-start.24
  204.9 715.5 %all-gather.25.cloned.1.call-start = ((), (), s32[]{:S(2)}) async-start(), calls=%async_computation.21 | async-start | bytes 8650752 | tf_op jit(solution)/shard_map/all_gather | solution.py:156
  205.7 859.5 %all-gather.29.cloned.1.call-start = ((), (), s32[]{:S(2)}) async-start(), calls=%async_computation.23 | async-start | bytes 28835840 | tf_op jit(solution)/shard_map/all_gather | solution.py:241
  240.5 969.3 %all-gather.33.cloned.1.call-start = ((), (), s32[]{:S(2)}) async-start(), calls=%async_computation.25 | async-start | bytes 28835840 | tf_op jit(solution)/shard_map/all_gather | solution.py:242
  333.4 93.7 %copy-start.64 = (u32[32]{0:T(128)S(1)}, u32[32]{0:T(128)}, u32[]{:S(2)}) copy-start(u32[32]{0:T(128)} %constant.117) | copy-start | bytes 388
  333.4 1021.2 %all-gather.37.cloned.1.call-start = ((), (), s32[]{:S(2)}) async-start(), calls=%async_computation.27 | async-start | bytes 28835840 | tf_op jit(solution)/shard_map/all_gather | solution.py:243
  484.6 42.9 %all-to-all-start = ((bf16[4,2,8192]{2,1,0:T(2,128)(2,1)}), bf16[4,2,8192]{2,1,0:T(2,128)(2,1)S(1)}, u32[]{:S(2)}, u32[]{:S(2)}) async-start(bf16[4,2,8192]{2,1,0:T(2,128)(2,1)} %reshape.352), calls=%async_computation | async-start | bytes 262144 | tf_op jit(solution)/shard_map/all_to_all | solution.py:187
  531.5 45.9 %copy-start.37 = (bf16[4,256,4,16]{1,3,2,0:T(8,128)(2,1)}, bf16[4,256,4,16]{1,3,2,0:T(8,128)(2,1)S(1)}, u32[]{:S(2)}) copy-start(bf16[4,256,4,16]{1,3,2,0:T(8,128)(2,1)S(1)} %reshape.279) | copy-start | bytes 393220
  531.5 45.9 %copy-start.33 = (f32[4,256,256]{1,2,0:T(8,128)S(1)}, f32[4,256,256]{1,2,0:T(8,128)}, u32[]{:S(2)}) copy-start(f32[4,256,256]{1,2,0:T(8,128)} %and_convert_fusion) | copy-start | bytes 3145732
  531.6 45.9 %copy-start.40 = (bf16[4,256,4,16]{1,3,2,0:T(8,128)(2,1)S(1)}, bf16[4,256,4,16]{1,3,2,0:T(8,128)(2,1)}, u32[]{:S(2)}) copy-start(bf16[4,256,4,16]{1,3,2,0:T(8,128)(2,1)} %copy-done.39) | copy-start | bytes 393220
  881.6 27.8 all-to-all-start.3
  885.1 708.3 %reduce-scatter.31.cloned.1.call-start = ((), (), s32[]{:S(2)}) async-start(), calls=%async_computation.38 | async-start | bytes 28835840
  926.6 577.5 %copy-start.14 = (f32[256,2048]{1,0:T(8,128)}, f32[256,2048]{1,0:T(8,128)S(1)}, u32[]{:S(2)}) copy-start(f32[256,2048]{1,0:T(8,128)S(1)} %get-tuple-element.551) | copy-start | bytes 6291460
  1415.2 347.7 %reduce-scatter.33.cloned.1.call-start = ((), (), s32[]{:S(2)}) async-start(), calls=%async_computation.39 | async-start | bytes 28835840
  1463.0 469.2 %reduce-scatter.27.cloned.1.call-start = ((), (), s32[]{:S(2)}) async-start(), calls=%async_computation.34 | async-start | bytes 28835840 | tf_op jit(solution)/shard_map/reduce_scatter | solution.py:255
  1477.3 591.7 %all-gather.41.cloned.1.call-start = ((), (), s32[]{:S(2)}) async-start(), calls=%async_computation.37 | async-start | bytes 10063872 | tf_op jit(solution)/shard_map/all_gather | solution.py:35
  1568.4 681.6 %reduce-scatter.23.cloned.1.call-start = ((), (), s32[]{:S(2)}) async-start(), calls=%async_computation.32 | async-start | bytes 6488064 | tf_op jit(solution)/shard_map/reduce_scatter | solution.py:262
  1601.7 694.8 %reduce-scatter.25.cloned.1.call-start = ((), (), s32[]{:S(2)}) async-start(), calls=%async_computation.33 | async-start | bytes 6488064 | tf_op jit(solution)/shard_map/reduce_scatter | solution.py:265
  1771.4 160.9 %copy-start.3 = (bf16[4,1,1,64,2048]{4,3,2,1,0:T(8,128)(2,1)S(1)}, bf16[4,1,1,64,2048]{4,3,2,1,0:T(8,128)(2,1)}, u32[]{:S(2)}) copy-start(bf16[4,1,1,64,2048]{4,3,2,1,0:T(8,128)(2,1)} %param.16) | copy-start | bytes 3145732
  1771.4 160.9 %copy-start.49 = (f32[2048]{0:T(1024)S(1)}, f32[2048]{0:T(1024)}, u32[]{:S(2)}) copy-start(f32[2048]{0:T(1024)} %copy-done.48) | copy-start | bytes 24580
  1771.4 160.9 %copy-start.61 = (f32[4,64]{1,0:T(4,128)S(1)}, f32[4,64]{1,0:T(4,128)}, u32[]{:S(2)}) copy-start(f32[4,64]{1,0:T(4,128)} %copy-done.60) | copy-start | bytes 3076
  1771.4 162.3 %copy-start.55 = (f32[4]{0:T(128)S(1)}, f32[4]{0:T(128)}, u32[]{:S(2)}) copy-start(f32[4]{0:T(128)} %copy-done.54) | copy-start | bytes 52
  1771.4 639.3 %reduce-scatter.29.cloned.1.call-start = ((), (), s32[]{:S(2)}) async-start(), calls=%async_computation.35 | async-start | bytes 6488064 | tf_op jit(solution)/shard_map/reduce_scatter | solution.py:268
  1932.3 27.0 copy-start.45
  1976.9 51.5 %copy-start.7 = (bf16[4,1,1,64,2048]{4,3,2,1,0:T(8,128)(2,1)S(1)}, bf16[4,1,1,64,2048]{4,3,2,1,0:T(8,128)(2,1)}, u32[]{:S(2)}) copy-start(bf16[4,1,1,64,2048]{4,3,2,1,0:T(8,128)(2,1)} %multiply_convert_fusion.3) | copy-start | bytes 3145732
  1980.7 43.7 %all-to-all-start.5 = ((bf16[4,2,8192]{2,1,0:T(2,128)(2,1)}), bf16[4,2,8192]{2,1,0:T(2,128)(2,1)S(1)}, u32[]{:S(2)}, u32[]{:S(2)}) async-start(bf16[4,2,8192]{2,1,0:T(2,128)(2,1)} %reshape.356), calls=%async_computation.5 | async-start | bytes 262144 | tf_op jit(solution)/shard_map/all_to_all | solution.py:311
  1984.0 567.1 %reduce-scatter.15.cloned.1.call-start = ((), (), s32[]{:S(2)}) async-start(), calls=%async_computation.28 | async-start | bytes 2162688 | tf_op jit(solution)/shard_map/reduce_scatter | solution.py:328
  2028.3 40.7 %copy-start.42 = (bf16[256,256]{1,0:T(8,128)(2,1)}, bf16[256,256]{1,0:T(8,128)(2,1)S(1)}, u32[]{:S(2)}) copy-start(bf16[256,256]{1,0:T(8,128)(2,1)S(1)} %reshape.291) | copy-start | bytes 393220
  2030.2 657.9 %reduce-scatter.17.cloned.1.call-start = ((), (), s32[]{:S(2)}) async-start(), calls=%async_computation.29 | async-start | bytes 2162688 | tf_op jit(solution)/shard_map/reduce_scatter | solution.py:329
  2069.1 28.3 copy-start.53
  2125.3 920.2 %reduce-scatter.21.cloned.1.call-start = ((), (), s32[]{:S(2)}) async-start(), calls=%async_computation.31 | async-start | bytes 17301504 | tf_op jit(solution)/shard_map/reduce_scatter | solution.py:331
  2135.4 1270.5 %reduce-scatter.19.cloned.1.call-start = ((), (), s32[]{:S(2)}) async-start(), calls=%async_computation.30 | async-start | bytes 17301504 | tf_op jit(solution)/shard_map/reduce_scatter | solution.py:330
  2202.2 44.4 %copy-start.6 = (f32[256,2048]{1,0:T(8,128)S(1)}, f32[256,2048]{1,0:T(8,128)}, u32[]{:S(2)}) copy-start(f32[256,2048]{1,0:T(8,128)} %copy-done.5) | copy-start | bytes 6291460
  (44 other events, 297.3 us)
Sparse Core Ops, SparseCore 0:
  11.0 56.5 all-gather.20
  70.6 76.3 all-gather.22
  149.2 91.2 all-gather.26
  242.5 90.8 all-gather.30
  335.2 91.7 all-gather.34
  429.9 51.9 all-gather.18
  483.4 347.2 all-gather.38
  833.7 86.6 all-gather.24
  922.0 143.1 all-gather.28
  1066.6 143.1 all-gather.32
  1211.3 143.2 all-gather.36
  1415.4 178.0 reduce-scatter.30
  1596.2 166.7 reduce-scatter.32
  1765.4 166.7 reduce-scatter.26
  1935.1 133.9 all-gather.40
  2073.0 108.1 reduce-scatter.22
  2185.2 111.2 reduce-scatter.24
  2300.5 110.1 reduce-scatter.28
  2413.6 137.3 reduce-scatter.14
  2553.7 134.2 reduce-scatter.16
  2691.0 354.4 reduce-scatter.20
  3048.5 357.3 reduce-scatter.18
where the time goes:
time: 3420 us; the launch traced here: 3410 us
  waiting for transfers between devices  2580 us (75%)
  blocking collectives  271 us (8%)
  matrix products  253 us (7%)
  local copies, waits for them, and re-layouts  202 us (6%)
  other arithmetic  66 us (2%)
    reduce_scatter x1, waiting for transfers between devices, body(): lax.psum_scatter(value_sum, ('head', 'shard'), scatter_dimension=0, tiled...  360 us
    reduce_scatter x1, waiting for transfers between devices, body(): lax.psum_scatter(project_sum, ('head', 'shard'), scatter_dimension=0, til...  357 us
    all_gather x1, waiting for transfers between devices, carried_in(): everything = jax.tree.map(lambda part: lax.all_gather(part, axis), value)  246 us
    unnamed x24, waiting for transfers between devices  191 us
    dot_general x21, matrix products, product(): return jnp.dot(left, right, preferred_element_type=jnp.float32)  180 us
    reduce_scatter x1, waiting for transfers between devices, body(): lax.psum_scatter(down_whole.astype(jnp.bfloat16), 'head', scatter_dimensi...  161 us
    unnamed x4, blocking collectives  144 us
    all_gather x1, waiting for transfers between devices, body(): lax.all_gather(rows_gate, 'head', axis=1, tiled=True)  138 us
  transfers between devices with their start and end apart: 27, of which 24 were waited for; matrix products, arithmetic and copies ran while one was open for 13% of the time, Pallas kernels for 0%

commit v1 on v0

--- a/solution.py
+++ b/solution.py
@@ -10,6 +10,19 @@
 VD = 128
 EPS_NORM = 1e-05
 HIGH = lax.Precision.HIGHEST
+
+
+def ring_gather(array, axis, dim):
+    peers, place, rows = (lax.axis_size(axis), lax.axis_index(axis), array.shape[dim])
+    forward = [(i, (i + 1) % peers) for i in range(peers)]
+    filled = jnp.zeros((*array.shape[:dim], peers * rows, *array.shape[dim + 1 :]), array.dtype)
+    block = array
+    for turn in range(peers):
+        owner = (place - turn) % peers
+        filled = lax.dynamic_update_slice_in_dim(filled, block, owner * rows, axis=dim)
+        if turn < peers - 1:
+            block = lax.ppermute(block, axis, forward)
+    return filled
 
 
 def carried_in(value, axis, combine, identity):
@@ -240,7 +253,7 @@
     full_gate, full_up, full_down = (
         lax.all_gather(rows_gate, "head", axis=1, tiled=True),
         lax.all_gather(rows_up, "head", axis=1, tiled=True),
-        lax.all_gather(rows_down, "head", axis=0, tiled=True),
+        ring_gather(rows_down, "head", 0),
     )
     down_out, grad_active_two, gate_whole, up_whole, down_whole = swiglu_pass(
         active_two, grad_out, full_gate, full_up, full_down

time: 3420 us -> 3300 us (0.965)
  waiting for transfers between devices: 2580 us -> 2440 us
    all_gather x1 -> x0, waiting for transfers between devices: 131 us -> none  [body(): lax.all_gather(rows_down, 'head', axis=0, tiled=True)]
    ppermute x0 -> x3, waiting for transfers between devices: none -> 67.6 us  [ring_gather(): block = lax.ppermute(block, axis, forward)]
    all_gather x1, waiting for transfers between devices: 52.3 us -> 0.01 us  [body(): lax.all_gather(query_weight, ('head', 'shard'), axis=0, tiled=True)]
    all_gather x1, waiting for transfers between devices: 246 us -> 195 us  [carried_in(): everything = jax.tree.map(lambda part: lax.all_gather(part, axis), value)]
    unnamed x160 -> x166, local copies, waits for them, and re-layouts: 118 us -> 116 us
    unnamed x24 -> x23, waiting for transfers between devices: 191 us -> 191 us
  transfers between devices with their start and end apart: 27 -> 29, of which waited for: 24 -> 24; matrix products, arithmetic and copies ran while one was open for 13% -> 14% of each run, Pallas kernels for 0% -> 0%
where the time goes in v1:
time: 3300 us; the launch traced here: 3290 us
  waiting for transfers between devices  2440 us (74%)
  matrix products  263 us (8%)
  blocking collectives  258 us (8%)
  local copies, waits for them, and re-layouts  227 us (7%)
  other arithmetic  66 us (2%)
    reduce_scatter x1, waiting for transfers between devices, body(): lax.psum_scatter(value_sum, ('head', 'shard'), scatter_dimension=0, tiled...  360 us
    reduce_scatter x1, waiting for transfers between devices, body(): lax.psum_scatter(project_sum, ('head', 'shard'), scatter_dimension=0, til...  358 us
    all_gather x1, waiting for transfers between devices, carried_in(): everything = jax.tree.map(lambda part: lax.all_gather(part, axis), value)  195 us
    unnamed x23, waiting for transfers between devices  191 us
    dot_general x21, matrix products, product(): return jnp.dot(left, right, preferred_element_type=jnp.float32)  190 us
    reduce_scatter x1, waiting for transfers between devices, body(): lax.psum_scatter(down_whole.astype(jnp.bfloat16), 'head', scatter_dimensi...  161 us
    all_gather x1, waiting for transfers between devices, body(): lax.all_gather(rows_gate, 'head', axis=1, tiled=True)  138 us
    reduce_scatter x1, waiting for transfers between devices, body(): lax.psum_scatter(query_sum, ('head', 'shard'), scatter_dimension=0, tiled...  138 us
  transfers between devices with their start and end apart: 29, of which 24 were waited for; matrix products, arithmetic and copies ran while one was open for 14% of the time, Pallas kernels for 0%

profile of v1, /device:TPU:0, one launch (start us, length us, event | category | flops | bytes accessed | tf_op | source)
XLA Modules:
  0.0 3293.1 jit_solution(14430680303624253717)
XLA Ops:
  12.9 42.1 %all-reduce.7 = (bf16[2048]{0:T(1024)(128)(2,1)S(1)}, bf16[2048]{0:T(1024)(128)(2,1)S(1)}) all-reduce(bf16[2048]{0:T(1024)(128)(2,1)S(1)} %dynamic-update-slice, bf16[2048]{0:T(1024)(128)(2,1)S(1)} %dynamic-update-slice.2), channel_id=1, replica_groups=mesh['head'=4,'shard'=8] {'head','shard'}, use_global_device_ids=true, to_apply=%add | all-reduce | flops 4096 | bytes 16384
  58.5 9.1 all-gather.20.cloned.1.call-done
  78.9 68.0 %all-gather.22.cloned.1.call-done = bf16[2048,2048]{1,0:T(8,128)(2,1)} async-done(((bf16[64,2048]{1,0:T(8,128)(2,1)}), bf16[2048,2048]{1,0:T(8,128)(2,1)}) %all-gather.22.cloned.1.call-update) | async-done | bytes 8388624 | tf_op jit(solution)/shard_map/all_gather | solution.py:168
  166.9 11.5 all-to-all-done.2
  203.1 37.4 %all-gather.26.cloned.1.call-done = bf16[2048,1408]{1,0:T(8,128)(2,1)} async-done(((bf16[256,1408]{1,0:T(8,128)(2,1)}), bf16[2048,1408]{1,0:T(8,128)(2,1)}) %all-gather.26.cloned.1.call-update) | async-done | bytes 5767184 | tf_op jit(solution)/shard_map/all_gather | solution.py:245
  240.5 92.8 %all-gather.30.cloned.1.call-done = bf16[2048,1408]{1,0:T(8,128)(2,1)} async-done(((bf16[256,1408]{1,0:T(8,128)(2,1)}), bf16[2048,1408]{1,0:T(8,128)(2,1)}) %all-gather.30.cloned.1.call-update) | async-done | bytes 5767184 | tf_op jit(solution)/shard_map/all_gather | solution.py:246
  333.4 93.7 %all-gather.34.cloned.1.call-done = bf16[1408,2048]{1,0:T(8,128)(2,1)} async-done(((bf16[1408,256]{1,0:T(8,128)(2,1)}), bf16[1408,2048]{1,0:T(8,128)(2,1)}) %all-gather.34.cloned.1.call-update) | async-done | bytes 5767184 | tf_op jit(solution)/shard_map/all_gather | solution.py:247
  427.0 67.6 %collective-permute-done = bf16[1408,2048]{1,0:T(8,128)(2,1)} collective-permute-done((bf16[1408,2048]{1,0:T(8,128)(2,1)}, bf16[1408,2048]{1,0:T(8,128)(2,1)}, u32[]{:S(2)}, u32[]{:S(2)}) %collective-permute-start) | collective-permute-done | bytes 5767200 | tf_op jit(solution)/shard_map/ppermute | solution.py:24
  503.9 23.9 all-reduce.1
  528.0 32.8 all-to-all-done
  569.6 41.0 %all-gather.2 = f32[32,4,273]{2,1,0:T(4,128)} all-gather(f32[4,4,273]{2,1,0:T(4,128)S(1)} %multiply_reduce_fusion), channel_id=4, replica_groups=mesh['head'=4,'shard'=8] {'shard'}, dimensions={0}, use_global_device_ids=true | all-gather | bytes 157248 | tf_op jit(solution)/shard_map/all_gather | solution.py:30
  636.3 194.9 %all-gather.36.cloned.1.call-done = f32[32,4,273,128]{3,1,2,0:T(4,128)} async-done(((f32[4,4,273,128]{3,1,2,0:T(4,128)}), f32[32,4,273,128]{3,1,2,0:T(4,128)}) %all-gather.36.cloned.1.call-update) | async-done | bytes 17891344 | tf_op jit(solution)/shard_map/all_gather | solution.py:30
  831.2 29.9 while.38
  867.8 8.5 fusion.18
  898.1 11.9 all-to-all-done.3
  912.1 9.1 all-gather.24.cloned.1.call-done
  927.6 138.3 %all-gather.28.cloned.1.call-done = bf16[2048,5632]{1,0:T(8,128)(2,1)} async-done(((bf16[2048,1408]{1,0:T(8,128)(2,1)}), bf16[2048,5632]{1,0:T(8,128)(2,1)}) %all-gather.28.cloned.1.call-update) | async-done | bytes 23068688 | tf_op jit(solution)/shard_map/all_gather | solution.py:254
  1065.9 14.4 fusion.61
  1080.3 130.2 %all-gather.32.cloned.1.call-done = bf16[2048,5632]{1,0:T(8,128)(2,1)} async-done(((bf16[2048,1408]{1,0:T(8,128)(2,1)}), bf16[2048,5632]{1,0:T(8,128)(2,1)}) %all-gather.32.cloned.1.call-update) | async-done | bytes 23068688 | tf_op jit(solution)/shard_map/all_gather | solution.py:255
  1210.5 13.2 fusion.62
  1223.7 27.6 multiply_convert_fusion
  1251.2 13.1 convolution_convert_fusion.2
  1264.3 30.7 copy.221
  1295.0 17.6 convolution_convert_fusion.1
  1312.6 30.2 copy.223
  1344.0 13.1 convolution_convert_fusion
  1357.2 13.2 fusion.63
  1370.3 13.6 multiply_reduce_fusion.5
  1396.0 29.4 all_to_all.114
  1448.1 25.1 reduce-scatter.31.cloned.1.call-done
  1481.5 161.0 %reduce-scatter.33.cloned.1.call-done = bf16[1408,2048]{1,0:T(8,128)(2,1)} async-done(((bf16[5632,2048]{1,0:T(8,128)(2,1)}), bf16[1408,2048]{1,0:T(8,128)(2,1)}) %reduce-scatter.33.cloned.1.call-update) | async-done | bytes 5767184
  1642.6 8.3 copy.224
  1651.0 160.9 %reduce-scatter.27.cloned.1.call-done = bf16[1408,2048]{1,0:T(8,128)(2,1)} async-done(((bf16[5632,2048]{1,0:T(8,128)(2,1)}), bf16[1408,2048]{1,0:T(8,128)(2,1)}) %reduce-scatter.27.cloned.1.call-update) | async-done | bytes 5767184 | tf_op jit(solution)/shard_map/reduce_scatter | solution.py:268
  1813.6 22.2 all-reduce.3
  1870.9 33.2 %all-gather.5 = bf16[32,4,273]{2,1,0:T(4,128)(2,1)} all-gather(bf16[4,4,273]{2,1,0:T(4,128)(2,1)S(1)} %bitcast.331), channel_id=7, replica_groups=mesh['head'=4,'shard'=8] {'shard'}, dimensions={0}, use_global_device_ids=true | all-gather | bytes 78624 | tf_op jit(solution)/shard_map/all_gather | solution.py:48
  1910.0 38.9 %all-gather.38.cloned.1.call-done = bf16[32,4,273,128]{3,1,2,0:T(4,128)(2,1)} async-done(((bf16[4,4,273,128]{3,1,2,0:T(4,128)(2,1)}), bf16[32,4,273,128]{3,1,2,0:T(4,128)(2,1)}) %all-gather.38.cloned.1.call-update) | async-done | bytes 8945680 | tf_op jit(solution)/shard_map/all_gather | solution.py:48
  1948.8 28.2 while.39
  2005.1 10.1 fusion.37
  2015.7 12.6 fusion.13
  2034.4 17.0 all_to_all.116
  2063.3 12.5 fusion.12
  2084.5 41.6 %all-reduce.6 = (f32[2048]{0:T(1024)S(1)}, f32[2048]{0:T(1024)S(1)}) all-reduce(f32[2048]{0:T(1024)S(1)} %get-tuple-element.499, f32[2048]{0:T(1024)S(1)} %get-tuple-element.497), channel_id=12, replica_groups=mesh['head'=4,'shard'=8] {'head','shard'}, use_global_device_ids=true, to_apply=%region_16.17.clone | all-reduce | flops 4096 | bytes 32768
  2133.1 43.4 %reduce-scatter.25.cloned.1.call-done = bf16[256,1408]{1,0:T(8,128)(2,1)} async-done(((bf16[2048,1408]{1,0:T(8,128)(2,1)}), bf16[256,1408]{1,0:T(8,128)(2,1)}) %reduce-scatter.25.cloned.1.call-update) | async-done | bytes 720912 | tf_op jit(solution)/shard_map/reduce_scatter | solution.py:278
  2178.8 111.8 %reduce-scatter.29.cloned.1.call-done = bf16[1408,256]{1,0:T(8,128)(2,1)} async-done(((bf16[1408,2048]{1,0:T(8,128)(2,1)}), bf16[1408,256]{1,0:T(8,128)(2,1)}) %reduce-scatter.29.cloned.1.call-update) | async-done | bytes 720912 | tf_op jit(solution)/shard_map/reduce_scatter | solution.py:281
  2292.9 137.8 %reduce-scatter.15.cloned.1.call-done = f32[64,256]{1,0:T(8,128)} async-done(((f32[2048,256]{1,0:T(8,128)}), f32[64,256]{1,0:T(8,128)}) %reduce-scatter.15.cloned.1.call-update) | async-done | bytes 65552 | tf_op jit(solution)/shard_map/reduce_scatter | solution.py:341
  2430.7 137.2 %reduce-scatter.17.cloned.1.call-done = f32[64,256]{1,0:T(8,128)} async-done(((f32[2048,256]{1,0:T(8,128)}), f32[64,256]{1,0:T(8,128)}) %reduce-scatter.17.cloned.1.call-update) | async-done | bytes 65552 | tf_op jit(solution)/shard_map/reduce_scatter | solution.py:342
  2567.9 357.9 %reduce-scatter.21.cloned.1.call-done = f32[64,2048]{1,0:T(8,128)} async-done(((f32[2048,2048]{1,0:T(8,128)}), f32[64,2048]{1,0:T(8,128)}) %reduce-scatter.21.cloned.1.call-update) | async-done | bytes 524304 | tf_op jit(solution)/shard_map/reduce_scatter | solution.py:344
  2925.8 360.3 %reduce-scatter.19.cloned.1.call-done = f32[64,2048]{1,0:T(8,128)} async-done(((f32[2048,2048]{1,0:T(8,128)}), f32[64,2048]{1,0:T(8,128)}) %reduce-scatter.19.cloned.1.call-update) | async-done | bytes 524304 | tf_op jit(solution)/shard_map/reduce_scatter | solution.py:343
  (411 shorter events, 355.6 us)
Async XLA Ops:
  7.2 51.0 %copy-start.2 = (bf16[4,1,1,64,2048]{4,3,2,1,0:T(8,128)(2,1)S(1)}, bf16[4,1,1,64,2048]{4,3,2,1,0:T(8,128)(2,1)}, u32[]{:S(2)}) copy-start(bf16[4,1,1,64,2048]{4,3,2,1,0:T(8,128)(2,1)} %param.16) | copy-start | bytes 3145732
  7.2 60.4 %all-gather.20.cloned.1.call-start = ((), (), s32[]{:S(2)}) async-start(), calls=%async_computation.19 | async-start | bytes 1081344 | tf_op jit(solution)/shard_map/all_gather | solution.py:167
  7.9 139.1 %all-gather.22.cloned.1.call-start = ((), (), s32[]{:S(2)}) async-start(), calls=%async_computation.20 | async-start | bytes 8650752 | tf_op jit(solution)/shard_map/all_gather | solution.py:168
  8.7 231.8 %all-gather.26.cloned.1.call-start = ((), (), s32[]{:S(2)}) async-start(), calls=%async_computation.22 | async-start | bytes 6488064 | tf_op jit(solution)/shard_map/all_gather | solution.py:245
  9.4 323.9 %all-gather.30.cloned.1.call-start = ((), (), s32[]{:S(2)}) async-start(), calls=%async_computation.24 | async-start | bytes 6488064 | tf_op jit(solution)/shard_map/all_gather | solution.py:246
  10.0 417.0 %all-gather.34.cloned.1.call-start = ((), (), s32[]{:S(2)}) async-start(), calls=%async_computation.26 | async-start | bytes 6488064 | tf_op jit(solution)/shard_map/all_gather | solution.py:247
  10.6 486.5 %all-gather.18.cloned.1.call-start = ((), (), s32[]{:S(2)}) async-start(), calls=%async_computation.18 | async-start | bytes 1081344 | tf_op jit(solution)/shard_map/all_gather | solution.py:166
  70.3 7.9 all-to-all-start.1
  73.8 492.5 %copy-start.51 = (f32[4,256]{1,0:T(4,128)}, f32[4,256]{1,0:T(4,128)S(1)}, u32[]{:S(2)}) copy-start(f32[4,256]{1,0:T(4,128)S(1)} %compare_convert_fusion.3) | copy-start | bytes 12292
  73.8 794.0 %copy-start.57 = (f32[273]{0:T(512)}, f32[273]{0:T(512)S(1)}, u32[]{:S(2)}) copy-start(f32[273]{0:T(512)S(1)} %pad.3.clone) | copy-start | bytes 3280
  78.9 535.1 %copy-start.37 = (bf16[4,256,4,16]{1,3,2,0:T(8,128)(2,1)}, bf16[4,256,4,16]{1,3,2,0:T(8,128)(2,1)S(1)}, u32[]{:S(2)}) copy-start(bf16[4,256,4,16]{1,3,2,0:T(8,128)(2,1)S(1)} %reshape.281) | copy-start | bytes 393220
  159.6 18.8 all-to-all-start.2
  163.9 667.3 %all-gather.36.cloned.1.call-start = ((), (), s32[]{:S(2)}) async-start(), calls=%async_computation.35 | async-start | bytes 20127744 | tf_op jit(solution)/shard_map/all_gather | solution.py:30
  164.3 30.5 copy-start.25
  202.3 718.9 %all-gather.24.cloned.1.call-start = ((), (), s32[]{:S(2)}) async-start(), calls=%async_computation.21 | async-start | bytes 8650752 | tf_op jit(solution)/shard_map/all_gather | solution.py:169
  203.0 862.9 %all-gather.28.cloned.1.call-start = ((), (), s32[]{:S(2)}) async-start(), calls=%async_computation.23 | async-start | bytes 28835840 | tf_op jit(solution)/shard_map/all_gather | solution.py:254
  240.5 254.2 %copy-start.65 = (u32[32]{0:T(128)S(1)}, u32[32]{0:T(128)}, u32[]{:S(2)}) copy-start(u32[32]{0:T(128)} %constant.160) | copy-start | bytes 388
  240.5 970.0 %all-gather.32.cloned.1.call-start = ((), (), s32[]{:S(2)}) async-start(), calls=%async_computation.25 | async-start | bytes 28835840 | tf_op jit(solution)/shard_map/all_gather | solution.py:255
  333.3 170.5 %copy-start.64 = (f32[4,1]{0,1:T(1,128)S(1)}, f32[4,1]{0,1:T(1,128)}, u32[]{:S(2)}) copy-start(f32[4,1]{0,1:T(1,128)} %copy-done.63) | copy-start | bytes 52
  427.0 67.6 %collective-permute-start = (bf16[1408,2048]{1,0:T(8,128)(2,1)}, bf16[1408,2048]{1,0:T(8,128)(2,1)}, u32[]{:S(2)}, u32[]{:S(2)}) collective-permute-start(bf16[1408,2048]{1,0:T(8,128)(2,1)} %all-gather.34.cloned.1.call-done), channel_id=1, source_target_pairs={{0,8},{8,16},{16,24},{24,0},{1,9},{9,17},{17,25},{25,1},{2,10},{10... | collective-permute-start | bytes 17301512 | tf_op jit(solution)/shard_map/ppermute | solution.py:24
  494.6 141.5 %collective-permute-start.1 = (bf16[1408,2048]{1,0:T(8,128)(2,1)}, bf16[1408,2048]{1,0:T(8,128)(2,1)}, u32[]{:S(2)}, u32[]{:S(2)}) collective-permute-start(bf16[1408,2048]{1,0:T(8,128)(2,1)} %collective-permute-done), channel_id=1, source_target_pairs={{0,8},{8,16},{16,24},{24,0},{1,9},{9,17},{17,25},{25,1},{2,10},{10... | collective-permute-start | bytes 17301512 | tf_op jit(solution)/shard_map/ppermute | solution.py:24
  499.8 60.9 %all-to-all-start = ((bf16[4,2,8192]{2,1,0:T(2,128)(2,1)}), bf16[4,2,8192]{2,1,0:T(2,128)(2,1)}, u32[]{:S(2)}, u32[]{:S(2)}) async-start(bf16[4,2,8192]{2,1,0:T(2,128)(2,1)} %reshape.352), calls=%async_computation | async-start | bytes 262144 | tf_op jit(solution)/shard_map/all_to_all | solution.py:200
  566.3 44.3 %copy-start.39 = (bf16[4,256,4,16]{1,3,2,0:T(8,128)(2,1)S(1)}, bf16[4,256,4,16]{1,3,2,0:T(8,128)(2,1)}, u32[]{:S(2)}) copy-start(bf16[4,256,4,16]{1,3,2,0:T(8,128)(2,1)} %reshape.279) | copy-start | bytes 393220
  566.3 47.7 %copy-start.34 = (f32[4,256,256]{1,2,0:T(8,128)S(1)}, f32[4,256,256]{1,2,0:T(8,128)}, u32[]{:S(2)}) copy-start(f32[4,256,256]{1,2,0:T(8,128)} %and_convert_fusion) | copy-start | bytes 3145732
  636.1 255.8 %collective-permute-start.2 = (bf16[1408,2048]{1,0:T(8,128)(2,1)}, bf16[1408,2048]{1,0:T(8,128)(2,1)}, u32[]{:S(2)}, u32[]{:S(2)}) collective-permute-start(bf16[1408,2048]{1,0:T(8,128)(2,1)} %collective-permute-done.1), channel_id=1, source_target_pairs={{0,8},{8,16},{16,24},{24,0},{1,9},{9,17},{17,25},{25,1},{2,10},{10... | collective-permute-start | bytes 17301512 | tf_op jit(solution)/shard_map/ppermute | solution.py:24
  882.1 27.9 all-to-all-start.3
  885.6 587.6 %reduce-scatter.31.cloned.1.call-start = ((), (), s32[]{:S(2)}) async-start(), calls=%async_computation.37 | async-start | bytes 28835840
  927.4 456.6 %copy-start.14 = (f32[256,2048]{1,0:T(8,128)}, f32[256,2048]{1,0:T(8,128)S(1)}, u32[]{:S(2)}) copy-start(f32[256,2048]{1,0:T(8,128)S(1)} %get-tuple-element.551) | copy-start | bytes 6291460
  1295.0 347.6 %reduce-scatter.33.cloned.1.call-start = ((), (), s32[]{:S(2)}) async-start(), calls=%async_computation.38 | async-start | bytes 28835840
  1342.8 469.2 %reduce-scatter.27.cloned.1.call-start = ((), (), s32[]{:S(2)}) async-start(), calls=%async_computation.33 | async-start | bytes 28835840 | tf_op jit(solution)/shard_map/reduce_scatter | solution.py:268
  1357.1 591.7 %all-gather.38.cloned.1.call-start = ((), (), s32[]{:S(2)}) async-start(), calls=%async_computation.36 | async-start | bytes 10063872 | tf_op jit(solution)/shard_map/all_gather | solution.py:48
  1448.0 682.7 %reduce-scatter.23.cloned.1.call-start = ((), (), s32[]{:S(2)}) async-start(), calls=%async_computation.31 | async-start | bytes 6488064 | tf_op jit(solution)/shard_map/reduce_scatter | solution.py:275
  1481.5 695.0 %reduce-scatter.25.cloned.1.call-start = ((), (), s32[]{:S(2)}) async-start(), calls=%async_computation.32 | async-start | bytes 6488064 | tf_op jit(solution)/shard_map/reduce_scatter | solution.py:278
  1650.9 161.1 %copy-start.3 = (bf16[4,1,1,64,2048]{4,3,2,1,0:T(8,128)(2,1)S(1)}, bf16[4,1,1,64,2048]{4,3,2,1,0:T(8,128)(2,1)}, u32[]{:S(2)}) copy-start(bf16[4,1,1,64,2048]{4,3,2,1,0:T(8,128)(2,1)} %param.16) | copy-start | bytes 3145732
  1651.0 161.1 %copy-start.48 = (f32[2048]{0:T(1024)S(1)}, f32[2048]{0:T(1024)}, u32[]{:S(2)}) copy-start(f32[2048]{0:T(1024)} %copy-done.47) | copy-start | bytes 24580
  1651.0 161.1 %copy-start.60 = (f32[4,64]{1,0:T(4,128)S(1)}, f32[4,64]{1,0:T(4,128)}, u32[]{:S(2)}) copy-start(f32[4,64]{1,0:T(4,128)} %copy-done.59) | copy-start | bytes 3076
  1651.0 162.4 %copy-start.54 = (f32[4]{0:T(128)S(1)}, f32[4]{0:T(128)}, u32[]{:S(2)}) copy-start(f32[4]{0:T(128)} %copy-done.53) | copy-start | bytes 52
  1651.0 639.6 %reduce-scatter.29.cloned.1.call-start = ((), (), s32[]{:S(2)}) async-start(), calls=%async_computation.34 | async-start | bytes 6488064 | tf_op jit(solution)/shard_map/reduce_scatter | solution.py:281
  1812.0 27.4 copy-start.44
  1857.0 51.1 %copy-start.7 = (bf16[4,1,1,64,2048]{4,3,2,1,0:T(8,128)(2,1)S(1)}, bf16[4,1,1,64,2048]{4,3,2,1,0:T(8,128)(2,1)}, u32[]{:S(2)}) copy-start(bf16[4,1,1,64,2048]{4,3,2,1,0:T(8,128)(2,1)} %multiply_convert_fusion.3) | copy-start | bytes 3145732
  1860.7 43.4 %all-to-all-start.5 = ((bf16[4,2,8192]{2,1,0:T(2,128)(2,1)}), bf16[4,2,8192]{2,1,0:T(2,128)(2,1)S(1)}, u32[]{:S(2)}, u32[]{:S(2)}) async-start(bf16[4,2,8192]{2,1,0:T(2,128)(2,1)} %reshape.356), calls=%async_computation.5 | async-start | bytes 262144 | tf_op jit(solution)/shard_map/all_to_all | solution.py:324
  1864.1 566.6 %reduce-scatter.15.cloned.1.call-start = ((), (), s32[]{:S(2)}) async-start(), calls=%async_computation.27 | async-start | bytes 2162688 | tf_op jit(solution)/shard_map/reduce_scatter | solution.py:341
  1908.1 40.8 %copy-start.41 = (bf16[256,256]{1,0:T(8,128)(2,1)}, bf16[256,256]{1,0:T(8,128)(2,1)S(1)}, u32[]{:S(2)}) copy-start(bf16[256,256]{1,0:T(8,128)(2,1)S(1)} %reshape.291) | copy-start | bytes 393220
  1909.9 658.0 %reduce-scatter.17.cloned.1.call-start = ((), (), s32[]{:S(2)}) async-start(), calls=%async_computation.28 | async-start | bytes 2162688 | tf_op jit(solution)/shard_map/reduce_scatter | solution.py:342
  1948.8 28.3 copy-start.52
  2005.1 920.7 %reduce-scatter.21.cloned.1.call-start = ((), (), s32[]{:S(2)}) async-start(), calls=%async_computation.30 | async-start | bytes 17301504 | tf_op jit(solution)/shard_map/reduce_scatter | solution.py:344
  2015.2 1270.9 %reduce-scatter.19.cloned.1.call-start = ((), (), s32[]{:S(2)}) async-start(), calls=%async_computation.29 | async-start | bytes 17301504 | tf_op jit(solution)/shard_map/reduce_scatter | solution.py:343
  2082.3 45.0 %copy-start.6 = (f32[256,2048]{1,0:T(8,128)S(1)}, f32[256,2048]{1,0:T(8,128)}, u32[]{:S(2)}) copy-start(f32[256,2048]{1,0:T(8,128)} %copy-done.5) | copy-start | bytes 6291460
  (49 other events, 403.7 us)
Sparse Core Ops, SparseCore 0:
  11.0 56.5 all-gather.19
  70.6 76.3 all-gather.21
  149.2 91.2 all-gather.25
  242.5 90.8 all-gather.29
  335.2 91.7 all-gather.33
  429.9 52.4 all-gather.17
  483.9 347.2 all-gather.35
  834.2 86.9 all-gather.23
  922.7 143.0 all-gather.27
  1067.3 143.1 all-gather.31
  1295.1 178.0 reduce-scatter.30
  1475.8 166.7 reduce-scatter.32
  1645.2 166.7 reduce-scatter.26
  1814.8 133.9 all-gather.37
  1952.8 108.2 reduce-scatter.22
  2065.0 111.4 reduce-scatter.24
  2180.4 110.1 reduce-scatter.28
  2293.4 137.2 reduce-scatter.14
  2433.5 134.2 reduce-scatter.16
  2570.7 355.0 reduce-scatter.20
  2928.7 357.3 reduce-scatter.18
